TPU v7x, 32 devices: a whole 2x2x4 slice. The times are simulated.
32 devices in a mesh: member: 2 (over y), tile: 4 (over z), day: 4 (over x, core).
Axes of the slice: x: 2, y: 2, z: 4, core: 2. Of those that a mesh axis runs over, the one named last changes fastest.
Arguments:
- fields: bfloat16 [64, 35, 16384], P(('member', 'day'), None, 'tile'), parts along dimension 0, may hold values from -6 to 6
- remap_tiles: bfloat16 [512, 128, 128], P('tile'), may hold values from 0 to 0.015625
- tile_source: int32 [512], P('tile'), may hold values from 0 to 31, as said below
- tile_band: int32 [512, 1], P('tile'), may hold values from 0 to 3, as said below
- tile_block: int32 [512], P('tile'), may hold values from 0 to 35, as said below
- patterns: bfloat16 [18432, 512], P('tile'), may hold values from -0.125 to 0.125
Outputs:
- scores: float32 [64, 35, 512], P(('member', 'day'), None, 'tile'), parts along dimension 0
There are 2 independent parts, one for each index of `member`. A program takes and returns all parts, laid end to end along the dimension named above; an argument that names none is the same for every part. Nothing has to cross between parts.
Inputs may be any that keep to these rules, and one draw needn't show every extreme that they name: `tile_source`: index of the source block, among the 32 blocks held by the tile's own device; each of those blocks is read by some tile of that device. `tile_band`: among the 128 tiles of one device, at most 64 go to one band, and in some device exactly 64 do. `tile_block`: every target block of every band is written by at least one tile.
All inputs are finite; a program needn't handle non-finite values.
Results may differ from a plain program's by a relative error of at most 0.0039.
Values may be sent and summed in bfloat16 or wider, within the bound.
No kernel may reach another device: no remote copies, remote signals or barrier semaphores. Data moves between devices by JAX's collectives and lax.ppermute only.
A program may use at most 128 MiB of HBM per device.

v0:
```python
import jax
import jax.numpy as jnp
from jax import lax
from jax.sharding import PartitionSpec as P


def on_device(fields, remap_tiles, tile_source, tile_band, tile_block, patterns):
    band_count = lax.axis_size("tile")
    day_count, var_count, source_cells = fields.shape
    tile_count, block_size, _ = remap_tiles.shape
    row_count = day_count * var_count
    source_blocks = source_cells // block_size
    target_blocks = patterns.shape[0] // block_size
    pattern_count = patterns.shape[1]
    pattern_share = pattern_count // band_count
    capacity = max(2, 2 * tile_count // band_count)
    slot_count = band_count * capacity
    blocked = fields.reshape(row_count, source_blocks, block_size)
    columns = jnp.take(blocked, tile_source, axis=1)
    owner = tile_band[:, 0]
    tile_order = jnp.arange(tile_count, dtype=jnp.int32)
    same_owner = owner[:, None] == owner[None, :]
    earlier = tile_order[:, None] > tile_order[None, :]
    rank_within = jnp.sum(jnp.logical_and(same_owner, earlier).astype(jnp.int32), axis=1)
    slot_index = owner * capacity + rank_within
    block_label = (
        jnp.full((slot_count,), -1.0, jnp.bfloat16)
        .at[slot_index]
        .set(tile_block.astype(jnp.bfloat16))
    )
    contrib = jnp.einsum(
        "rtk,tkj->trj", columns, remap_tiles, preferred_element_type=jnp.float32
    ).astype(jnp.bfloat16)
    send_values = (
        jnp.zeros((slot_count, row_count, block_size), jnp.bfloat16).at[slot_index].set(contrib)
    )
    received, label_recv = (
        lax.all_to_all(send_values, "tile", split_axis=0, concat_axis=0, tiled=True),
        lax.all_to_all(block_label, "tile", split_axis=0, concat_axis=0, tiled=True),
    )
    block_ids = jnp.arange(target_blocks, dtype=jnp.int32).astype(jnp.bfloat16)
    selector = (label_recv[None, :] == block_ids[:, None]).astype(jnp.bfloat16)
    remapped = jnp.einsum("bs,srk->rbk", selector, received, preferred_element_type=jnp.float32)
    remapped = remapped.astype(jnp.bfloat16).reshape(row_count, target_blocks * block_size)
    partial_scores = jnp.dot(remapped, patterns, preferred_element_type=jnp.float32)
    total_scores = lax.psum(partial_scores, "tile")
    own_scores = lax.dynamic_slice_in_dim(
        total_scores, lax.axis_index("tile") * pattern_share, pattern_share, 1
    )
    return own_scores.reshape(day_count, var_count, pattern_share)


def solution(mesh):
    return jax.shard_map(
        on_device,
        mesh=mesh,
        in_specs=(
            P(("member", "day"), None, "tile"),
            P("tile", None, None),
            P("tile"),
            P("tile", None),
            P("tile"),
            P("tile", None),
        ),
        out_specs=P(("member", "day"), None, "tile"),
        check_vma=False,
    )
```

profile of v0, /device:TPU:0, one launch (start us, length us, event | category | flops | bytes accessed | tf_op | source)
XLA Modules:
  0.0 542.6 jit_solution(3007958193052604485)
XLA Ops:
  6.5 0.9 convert_reduce_fusion
  7.4 0.7 fusion.21
  8.1 0.7 convert_element_type.25
  8.8 1.3 scatter_custom_fusion.1
  10.1 0.7 all_to_all.12
  10.8 6.3 %all-to-all-start.1 = ((bf16[4,64,1]{1,2,0:T(2,128)(2,1)}), bf16[4,64,1]{1,2,0:T(2,128)(2,1)S(1)}, u32[]{:S(2)}, u32[]{:S(2)}) async-start(bf16[4,64,1]{1,2,0:T(2,128)(2,1)} %all_to_all.12), calls=%async_computation.1 | async-start | bytes 4096 | tf_op jit(solution)/shard_map/all_to_all | solution.py:39
  17.1 0.7 compare_select_fusion
  17.8 0.7 compare_and_fusion
  18.4 2.9 copy.16
  21.4 2.6 reshape.24
  24.0 2.5 copy.17
  26.5 7.1 %gather_fusion = bf16[128,280,128]{2,1,0:T(8,128)(2,1)} fusion(bf16[280,32,128]{2,0,1:T(8,128)(2,1)S(1)} %copy.17, s32[1024]{0:T(1024)S(1)} %pad_clamp_fusion), kind=kCustom, calls=%fused_computation | custom fusion | bytes 18350592 | tf_op jit(solution)/shard_map/jit(_take)/gather | solution.py:19
  33.6 13.4 %fusion.6 = bf16[128,280,128]{2,1,0:T(8,128)(2,1)} fusion(bf16[128,128,128]{2,1,0:T(8,128)(2,1)} %param.7, bf16[128,280,128]{2,1,0:T(8,128)(2,1)} %gather_fusion, pred[128]{0:T(512)(128)(4,1)S(1)} %compare_and_fusion), kind=kOutput, calls=%fused_computation.9 | convolution fusion | flops 1183580160 | bytes 22544512 | tf_op jit(solution)/shard_map/rtk,tkj->trj/dot_general | solution.py:31
  47.0 6.6 %broadcast_in_dim.24 = bf16[256,280,128]{2,1,0:T(8,128)(2,1)} broadcast(bf16[]{:T(256)} %constant.12.clone.1), dimensions={} | broadcast | bytes 18350082 | tf_op jit(solution)/shard_map/broadcast_in_dim | solution.py:35
  53.5 24.0 %scatter_fusion = bf16[256,280,128]{2,1,0:T(8,128)(2,1)} fusion(bf16[256,280,128]{2,1,0:T(8,128)(2,1)} %broadcast_in_dim.24, s32[128]{0:T(128)S(1)} %fusion.21, bf16[128,280,128]{2,1,0:T(8,128)(2,1)} %fusion.6), kind=kCustom, calls=%fused_computation.1 | custom fusion | bytes 27525632 | tf_op jit(solution)/shard_map/scatter | solution.py:35
  77.5 0.0 all-to-all-done.1
  77.5 7.3 %all-to-all-start = ((bf16[256,280,128]{2,1,0:T(8,128)(2,1)}), bf16[256,280,128]{2,1,0:T(8,128)(2,1)}, u32[]{:S(2)}, u32[]{:S(2)}) async-start(bf16[256,280,128]{2,1,0:T(8,128)(2,1)} %scatter_fusion), calls=%async_computation | async-start | bytes 36700160 | tf_op jit(solution)/shard_map/all_to_all | solution.py:38
  84.8 0.2 all-reduce.2.cloned.1.call-start
  85.1 0.1 eq.34
  85.2 396.5 %all-to-all-done = bf16[256,280,128]{2,1,0:T(8,128)(2,1)} async-done(((bf16[256,280,128]{2,1,0:T(8,128)(2,1)}), bf16[256,280,128]{2,1,0:T(8,128)(2,1)}, u32[]{:S(2)}, u32[]{:S(2)}) %all-to-all-start) | async-done | bytes 18350112 | tf_op jit(solution)/shard_map/all_to_all | solution.py:38
  481.7 9.4 %fusion.13 = bf16[280,128,36]{1,2,0:T(8,128)(2,1)S(1)} fusion(bf16[256,280,128]{2,1,0:T(8,128)(2,1)} %all-to-all-done, bf16[256]{0:T(256)(128)(2,1)S(1)} %eq.34, bf16[36]{0:T(256)(128)(2,1)S(1)} %iota_convert_fusion), kind=kOutput, calls=%fused_computation.14 | convolution fusion | flops 661902336 | bytes 20931144 | tf_op jit(solution)/shard_map/bs,srk->rbk/dot_general | solution.py:43
  491.2 4.7 fusion.10
  495.8 0.0 all-reduce.2.cloned.1.call-update
  495.9 38.3 %all-reduce.2.cloned.1.call-done = f32[280,512]{1,0:T(8,128)} async-done(((f32[280,512]{1,0:T(8,128)}), f32[280,512]{1,0:T(8,128)}) %all-reduce.2.cloned.1.call-update) | async-done | bytes 573456 | tf_op jit(solution)/shard_map/psum | solution.py:46
  534.1 0.9 constant_dynamic-slice_fusion
  535.1 0.7 copy.20
  (4 shorter events, 0.0 us)
Async XLA Ops:
  10.8 66.7 %all-to-all-start.1 = ((bf16[4,64,1]{1,2,0:T(2,128)(2,1)}), bf16[4,64,1]{1,2,0:T(2,128)(2,1)S(1)}, u32[]{:S(2)}, u32[]{:S(2)}) async-start(bf16[4,64,1]{1,2,0:T(2,128)(2,1)} %all_to_all.12), calls=%async_computation.1 | async-start | bytes 4096 | tf_op jit(solution)/shard_map/all_to_all | solution.py:39
  77.5 404.2 %all-to-all-start = ((bf16[256,280,128]{2,1,0:T(8,128)(2,1)}), bf16[256,280,128]{2,1,0:T(8,128)(2,1)}, u32[]{:S(2)}, u32[]{:S(2)}) async-start(bf16[256,280,128]{2,1,0:T(8,128)(2,1)} %scatter_fusion), calls=%async_computation | async-start | bytes 36700160 | tf_op jit(solution)/shard_map/all_to_all | solution.py:38
  84.8 449.3 %all-reduce.2.cloned.1.call-start = ((), (), s32[]{:S(2)}) async-start(), calls=%async_computation.2 | async-start | bytes 1146880 | tf_op jit(solution)/shard_map/psum | solution.py:46
Sparse Core Ops, SparseCore 0:
  496.0 38.1 all-reduce.1
where the time goes:
time: 543 us
  waiting for transfers between devices  435 us (80%)
  local copies, waits for them, and re-layouts  49.4 us (9%)
  matrix products  27.5 us (5%)
  starting transfers between devices  13.8 us (3%)
  between operations  13.5 us (2%)
    all_to_all x1, waiting for transfers between devices, on_device(): lax.all_to_all(send_values, 'tile', split_axis=0, concat_axis=0, tiled=True)  397 us
    psum x1, waiting for transfers between devices, on_device(): total_scores = lax.psum(partial_scores, 'tile')  38.3 us
    scatter x1, local copies, waits for them, and re-layouts, on_device(): jnp.zeros((slot_count, row_count, block_size), jnp.bfloat16).at[slot_index]  24 us
    dot_general x1, matrix products, on_device(): jnp.einsum('rtk,tkj->trj', columns, remap_tiles, preferred_element_type=j...  13.4 us
  transfers between devices with their start and end apart: 3, of which 2 were waited for; matrix products, arithmetic and copies ran while one was open for 11% of the time, Pallas kernels for 0%

commit v1 on v0

--- a/solution.py
+++ b/solution.py
@@ -43,7 +43,11 @@
     remapped = jnp.einsum("bs,srk->rbk", selector, received, preferred_element_type=jnp.float32)
     remapped = remapped.astype(jnp.bfloat16).reshape(row_count, target_blocks * block_size)
     partial_scores = jnp.dot(remapped, patterns, preferred_element_type=jnp.float32)
-    total_scores = lax.psum(partial_scores, "tile")
+    total_scores = partial_scores
+    for hop in (1, 2):
+        total_scores = total_scores + lax.ppermute(
+            total_scores, "tile", [(dev, dev ^ hop) for dev in range(4)]
+        )
     own_scores = lax.dynamic_slice_in_dim(
         total_scores, lax.axis_index("tile") * pattern_share, pattern_share, 1
     )

time: 543 us -> 531 us (0.978)
  between operations: 13.5 us -> 0.11 us
    ppermute x0 -> x2, waiting for transfers between devices: none -> 40.3 us  [on_device(): lax.ppermute(total_scores, 'tile', [(dev, dev ^ hop) for dev in range(4)])]
    psum x1 -> x0, waiting for transfers between devices: 38.3 us -> none  [on_device(): total_scores = lax.psum(partial_scores, 'tile')]
  transfers between devices with their start and end apart: 3 -> 4, of which waited for: 2 -> 3; matrix products, arithmetic and copies ran while one was open for 11% -> 11% of each run, Pallas kernels for 0% -> 0%
where the time goes in v1:
time: 531 us; the launch traced here: 530 us
  waiting for transfers between devices  437 us (82%)
  local copies, waits for them, and re-layouts  48.5 us (9%)
  matrix products  26.7 us (5%)
  starting transfers between devices  13.9 us (3%)
    all_to_all x1, waiting for transfers between devices, on_device(): lax.all_to_all(send_values, 'tile', split_axis=0, concat_axis=0, tiled=True)  397 us
    ppermute x2, waiting for transfers between devices, on_device(): lax.ppermute(total_scores, 'tile', [(dev, dev ^ hop) for dev in range(4)])  40.3 us
    scatter x1, local copies, waits for them, and re-layouts, on_device(): jnp.zeros((slot_count, row_count, block_size), jnp.bfloat16).at[slot_index]  24 us
    dot_general x1, matrix products, on_device(): jnp.einsum('rtk,tkj->trj', columns, remap_tiles, preferred_element_type=j...  13.4 us
  transfers between devices with their start and end apart: 4, of which 3 were waited for; matrix products, arithmetic and copies ran while one was open for 11% of the time, Pallas kernels for 0%

profile of v1, /device:TPU:0, one launch (start us, length us, event | category | flops | bytes accessed | tf_op | source)
XLA Modules:
  0.0 530.0 jit_solution(2069957538258749205)
XLA Ops:
  0.0 0.9 convert_reduce_fusion
  0.9 0.7 fusion.21
  1.6 0.7 convert_element_type.25
  2.2 1.3 scatter_custom_fusion.1
  3.6 0.7 all_to_all.12
  4.2 6.3 %all-to-all-start.1 = ((bf16[4,64,1]{1,2,0:T(2,128)(2,1)}), bf16[4,64,1]{1,2,0:T(2,128)(2,1)S(1)}, u32[]{:S(2)}, u32[]{:S(2)}) async-start(bf16[4,64,1]{1,2,0:T(2,128)(2,1)} %all_to_all.12), calls=%async_computation.1 | async-start | bytes 4096 | tf_op jit(solution)/shard_map/all_to_all | solution.py:39
  10.6 0.7 compare_select_fusion
  11.2 0.7 compare_and_fusion
  11.9 2.9 copy.16
  14.8 2.6 reshape.24
  17.4 2.5 copy.17
  20.0 7.1 %gather_fusion = bf16[128,280,128]{2,1,0:T(8,128)(2,1)} fusion(bf16[280,32,128]{2,0,1:T(8,128)(2,1)S(1)} %copy.17, s32[1024]{0:T(1024)S(1)} %pad_clamp_fusion), kind=kCustom, calls=%fused_computation | custom fusion | bytes 18350592 | tf_op jit(solution)/shard_map/jit(_take)/gather | solution.py:19
  27.1 13.4 %fusion.6 = bf16[128,280,128]{2,1,0:T(8,128)(2,1)} fusion(bf16[128,128,128]{2,1,0:T(8,128)(2,1)} %param.7, bf16[128,280,128]{2,1,0:T(8,128)(2,1)} %gather_fusion, pred[128]{0:T(512)(128)(4,1)S(1)} %compare_and_fusion), kind=kOutput, calls=%fused_computation.9 | convolution fusion | flops 1183580160 | bytes 22544512 | tf_op jit(solution)/shard_map/rtk,tkj->trj/dot_general | solution.py:31
  40.4 6.6 %broadcast_in_dim.24 = bf16[256,280,128]{2,1,0:T(8,128)(2,1)} broadcast(bf16[]{:T(256)} %constant.12.clone.1), dimensions={} | broadcast | bytes 18350082 | tf_op jit(solution)/shard_map/broadcast_in_dim | solution.py:35
  47.0 24.0 %scatter_fusion = bf16[256,280,128]{2,1,0:T(8,128)(2,1)} fusion(bf16[256,280,128]{2,1,0:T(8,128)(2,1)} %broadcast_in_dim.24, s32[128]{0:T(128)S(1)} %fusion.21, bf16[128,280,128]{2,1,0:T(8,128)(2,1)} %fusion.6), kind=kCustom, calls=%fused_computation.1 | custom fusion | bytes 27525632 | tf_op jit(solution)/shard_map/scatter | solution.py:35
  71.0 0.0 all-to-all-done.1
  71.0 7.5 %all-to-all-start = ((bf16[256,280,128]{2,1,0:T(8,128)(2,1)}), bf16[256,280,128]{2,1,0:T(8,128)(2,1)}, u32[]{:S(2)}, u32[]{:S(2)}) async-start(bf16[256,280,128]{2,1,0:T(8,128)(2,1)} %scatter_fusion), calls=%async_computation | async-start | bytes 36700160 | tf_op jit(solution)/shard_map/all_to_all | solution.py:38
  78.5 0.1 eq.34
  78.6 396.8 %all-to-all-done = bf16[256,280,128]{2,1,0:T(8,128)(2,1)} async-done(((bf16[256,280,128]{2,1,0:T(8,128)(2,1)}), bf16[256,280,128]{2,1,0:T(8,128)(2,1)}, u32[]{:S(2)}, u32[]{:S(2)}) %all-to-all-start) | async-done | bytes 18350112 | tf_op jit(solution)/shard_map/all_to_all | solution.py:38
  475.4 9.4 %fusion.13 = bf16[280,128,36]{1,2,0:T(8,128)(2,1)S(1)} fusion(bf16[256,280,128]{2,1,0:T(8,128)(2,1)} %all-to-all-done, bf16[256]{0:T(256)(128)(2,1)S(1)} %eq.34, bf16[36]{0:T(256)(128)(2,1)S(1)} %iota_convert_fusion), kind=kOutput, calls=%fused_computation.14 | convolution fusion | flops 661902336 | bytes 20931144 | tf_op jit(solution)/shard_map/bs,srk->rbk/dot_general | solution.py:43
  484.8 3.8 fusion.10
  488.7 0.1 collective-permute-start
  488.7 14.0 %collective-permute-done = f32[280,512]{1,0:T(8,128)S(1)} collective-permute-done((f32[280,512]{1,0:T(8,128)S(1)}, f32[280,512]{1,0:T(8,128)S(1)}, u32[]{:S(2)}, u32[]{:S(2)}) %collective-permute-start) | collective-permute-done | bytes 573472 | tf_op jit(solution)/shard_map/ppermute | solution.py:48
  502.8 0.1 add.30
  502.8 0.1 collective-permute-start.1
  502.9 26.3 %collective-permute-done.1 = f32[280,512]{1,0:T(8,128)S(1)} collective-permute-done((f32[280,512]{1,0:T(8,128)S(1)}, f32[280,512]{1,0:T(8,128)S(1)}, u32[]{:S(2)}, u32[]{:S(2)}) %collective-permute-start.1) | collective-permute-done | bytes 573472 | tf_op jit(solution)/shard_map/ppermute | solution.py:48
  529.3 0.7 copy.20
  (5 shorter events, 0.1 us)
Async XLA Ops:
  4.2 66.7 %all-to-all-start.1 = ((bf16[4,64,1]{1,2,0:T(2,128)(2,1)}), bf16[4,64,1]{1,2,0:T(2,128)(2,1)S(1)}, u32[]{:S(2)}, u32[]{:S(2)}) async-start(bf16[4,64,1]{1,2,0:T(2,128)(2,1)} %all_to_all.12), calls=%async_computation.1 | async-start | bytes 4096 | tf_op jit(solution)/shard_map/all_to_all | solution.py:39
  71.0 404.4 %all-to-all-start = ((bf16[256,280,128]{2,1,0:T(8,128)(2,1)}), bf16[256,280,128]{2,1,0:T(8,128)(2,1)}, u32[]{:S(2)}, u32[]{:S(2)}) async-start(bf16[256,280,128]{2,1,0:T(8,128)(2,1)} %scatter_fusion), calls=%async_computation | async-start | bytes 36700160 | tf_op jit(solution)/shard_map/all_to_all | solution.py:38
  488.7 14.1 %collective-permute-start = (f32[280,512]{1,0:T(8,128)S(1)}, f32[280,512]{1,0:T(8,128)S(1)}, u32[]{:S(2)}, u32[]{:S(2)}) collective-permute-start(f32[280,512]{1,0:T(8,128)S(1)} %fusion.10), channel_id=1, source_target_pairs={{0,4},{4,0},{8,12},{12,8},{1,5},{5,1},{9,13},{13,9},{2,6},{6,2},{1... | collective-permute-start | bytes 1720328 | tf_op jit(solution)/shard_map/ppermute | solution.py:48
  502.8 26.4 %collective-permute-start.1 = (f32[280,512]{1,0:T(8,128)S(1)}, f32[280,512]{1,0:T(8,128)S(1)}, u32[]{:S(2)}, u32[]{:S(2)}) collective-permute-start(f32[280,512]{1,0:T(8,128)S(1)} %add.30), channel_id=1, source_target_pairs={{0,8},{4,12},{8,0},{12,4},{1,9},{5,13},{9,1},{13,5},{2,10},{6,14},... | collective-permute-start | bytes 1720328 | tf_op jit(solution)/shard_map/ppermute | solution.py:48
